TPU v7x, 128 devices: a whole 4x4x4 slice. The times are simulated.
128 devices in a mesh: wide: 16 (over x, z_hi, core), narrow: 8 (over z_lo, y).
Axes of the slice: x: 4, y: 4, z: 4 (z_hi: 2, z_lo: 2; z = z_hi * 2 + z_lo), core: 2. Of those that a mesh axis runs over, the one named last changes fastest.
Arguments:
- activations: bfloat16 [2048, 16384], P('wide', 'narrow'), may hold values from -30 to 30, as said below
- weight_tile: bfloat16 [16384, 16384], P('wide', 'narrow'), may hold values from -3 to 3
- codes: int32 [16384, 16384], P('wide', 'narrow'), may hold values from -8 to 7
- group_scales: float32 [16384, 128], P('wide', 'narrow'), may hold values from 0.02 to 0.2
- right_factor: bfloat16 [16384, 256], replicated, may hold values from -0.046875 to 0.046875
Outputs:
- residual_product: float32 [16384, 256], P(('wide', 'narrow'))
- gram: float32 [256, 256], replicated
- hessian_tiles: bfloat16 [16384, 16384], P('wide', 'narrow')
Inputs may be any that keep to these rules, and one draw needn't show every extreme that they name: `activations`: each token's features are a product of a token scale, a feature scale and a value.
All inputs are finite; a program needn't handle non-finite values.
Results may differ from a plain program's by a relative error of at most 0.0049.
Values may be sent and summed in bfloat16 or wider, within the bound.
A program may use at most 128 MiB of HBM per device.

v0:
```python
import jax
import jax.numpy as jnp
from jax import lax
from jax.sharding import PartitionSpec as P


def body(activations, weight_tile, codes, group_scales, right_factor):
    rows_local = weight_tile.shape[0]
    cols_local = weight_tile.shape[1]
    wide_count = lax.axis_size("wide")
    narrow_count = lax.axis_size("narrow")
    wide_index = lax.axis_index("wide")
    narrow_index = lax.axis_index("narrow")
    total_tokens = activations.shape[0] * wide_count
    contract_first = (((0,), (0,)), ((), ()))
    full_features = lax.all_gather(activations, "narrow", axis=1, tiled=True)
    row_operand = lax.all_to_all(full_features, "wide", split_axis=1, concat_axis=0, tiled=True)
    hess_sum = lax.dot_general(
        row_operand,
        lax.all_gather(activations, "wide", axis=0, tiled=True),
        contract_first,
        preferred_element_type=jnp.float32,
    )
    hessian = hess_sum / total_tokens
    hessian_tiles = hessian.astype(jnp.bfloat16)
    groups = group_scales.shape[1]
    width = cols_local // groups
    quantized = (
        codes.reshape(rows_local, groups, width).astype(jnp.float32) * group_scales[:, :, None]
    ).reshape(rows_local, cols_local)
    residual = (weight_tile.astype(jnp.float32) - quantized).astype(jnp.bfloat16)
    right_cols = lax.dynamic_slice_in_dim(right_factor, narrow_index * cols_local, cols_local, 0)
    partial_value = jnp.dot(
        hessian, right_cols.astype(jnp.float32), precision=lax.Precision.HIGHEST
    )
    product_own = lax.psum(partial_value, "narrow").astype(jnp.bfloat16)
    product_full = lax.all_gather(product_own, "wide", axis=0, tiled=True)
    product_cols = lax.dynamic_slice_in_dim(product_full, narrow_index * cols_local, cols_local, 0)
    share = rows_local // narrow_count
    gram_start = wide_index * rows_local + narrow_index * share
    product_share = lax.dynamic_slice_in_dim(product_full, gram_start, share, 0)
    right_share = lax.dynamic_slice_in_dim(right_factor, gram_start, share, 0)
    gram_part = lax.dot_general(
        right_share, product_share, contract_first, preferred_element_type=jnp.float32
    )
    gram = lax.psum(gram_part, ("wide", "narrow"))
    residual_product = lax.psum_scatter(
        jnp.dot(residual, product_cols, preferred_element_type=jnp.float32),
        "narrow",
        scatter_dimension=0,
        tiled=True,
    )
    return (residual_product, gram, hessian_tiles)


def solution(mesh):
    in_specs = (
        P("wide", "narrow"),
        P("wide", "narrow"),
        P("wide", "narrow"),
        P("wide", "narrow"),
        P(),
    )
    out_specs = (P(("wide", "narrow"), None), P(), P("wide", "narrow"))
    return jax.shard_map(body, mesh=mesh, in_specs=in_specs, out_specs=out_specs, check_vma=False)
```

profile of v0, /device:TPU:0, one launch (start us, length us, event | category | flops | bytes accessed | tf_op | source)
XLA Modules:
  0.0 524.6 jit_solution(170166573466252105)
XLA Ops:
  7.2 0.0 all-gather.4.cloned.1.call-start
  7.2 2.0 copy.11
  9.3 0.0 all-gather.4.cloned.1.call-update
  9.3 0.0 all-gather.6.cloned.1.call-start
  9.3 0.7 all-gather.6.cloned.1.call-update
  10.0 55.3 %all-gather.4.cloned.1.call-done = bf16[128,16384]{0,1:T(8,128)(2,1)} async-done(((bf16[128,2048]{0,1:T(8,128)(2,1)}), bf16[128,16384]{0,1:T(8,128)(2,1)}) %all-gather.4.cloned.1.call-update) | async-done | bytes 4194320 | tf_op jit(solution)/shard_map/all_gather | solution.py:16
  65.3 6.7 %all-to-all-start = ((bf16[128,16,1024]{0,2,1:T(8,128)(2,1)}), bf16[128,16,1024]{0,2,1:T(8,128)(2,1)}, u32[]{:S(2)}, u32[]{:S(2)}) async-start(bf16[128,16,1024]{0,2,1:T(8,128)(2,1)} %bitcast.14), calls=%async_computation | async-start | bytes 8388608 | tf_op jit(solution)/shard_map/all_to_all | solution.py:17
  72.0 0.0 all-gather.8.cloned.1.call-start
  72.1 63.8 %all-to-all-done = bf16[128,16,1024]{0,2,1:T(8,128)(2,1)} async-done(((bf16[128,16,1024]{0,2,1:T(8,128)(2,1)}), bf16[128,16,1024]{0,2,1:T(8,128)(2,1)}, u32[]{:S(2)}, u32[]{:S(2)}) %all-to-all-start) | async-done | bytes 4194336 | tf_op jit(solution)/shard_map/all_to_all | solution.py:17
  135.9 6.4 %copy.12 = bf16[16,128,1024]{2,1,0:T(8,128)(2,1)} copy(bf16[16,128,1024]{1,2,0:T(8,128)(2,1)} %bitcast.1) | data formatting | bytes 8388608 | tf_op jit(solution)/shard_map/all_to_all | solution.py:17
  142.3 29.6 %all-gather.6.cloned.1.call-done = bf16[2048,2048]{1,0:T(8,128)(2,1)} async-done(((bf16[128,2048]{1,0:T(8,128)(2,1)}), bf16[2048,2048]{1,0:T(8,128)(2,1)}) %all-gather.6.cloned.1.call-update) | async-done | bytes 8388624 | tf_op jit(solution)/shard_map/all_gather | solution.py:20
  171.8 14.3 %multiply_convert_fusion = (bf16[1024,2048]{1,0:T(8,128)(2,1)}, f32[1024,2048]{1,0:T(8,128)S(1)}) fusion(bf16[2048,1024]{1,0:T(8,128)(2,1)} %bitcast.15, bf16[2048,2048]{1,0:T(8,128)(2,1)} %all-gather.6.cloned.1.call-done), kind=kOutput, calls=%fused_computation.3 | convolution fusion | flops 8594128896 | bytes 25165824 | tf_op jit(solution)/shard_map/dot_general | solution.py:18
  186.2 0.0 copy-start.1
  186.2 5.3 %fusion.2 = f32[1024,256]{1,0:T(8,128)S(1)} fusion(f32[1024,2048]{1,0:T(8,128)S(1)} %get-tuple-element.4, bf16[16384,256]{1,0:T(8,128)(2,1)} %param.9, s32[]{:T(128)S(6)} %select_n.8), kind=kOutput, calls=%fused_computation.4 | convolution fusion | flops 6444548096 | bytes 10485764 | tf_op jit(solution)/shard_map/dot_general | solution.py:33
  191.4 67.2 %all-reduce.4 = bf16[1024,256]{1,0:T(8,128)(2,1)} all-reduce(f32[1024,256]{1,0:T(8,128)S(1)} %fusion.2), channel_id=1, replica_groups=mesh['wide'=16,'narrow'=8] {'narrow'}, use_global_device_ids=true, to_apply=%region_0.0 | all-reduce | flops 262144 | bytes 1572864 | tf_op jit(solution)/shard_map/psum | solution.py:36
  258.6 0.0 all-gather.8.cloned.1.call-update
  258.6 0.0 all-reduce.3.cloned.1.call-start
  258.7 0.0 copy-done.1
  258.7 0.2 copy.10
  258.9 71.8 %all-gather.8.cloned.1.call-done = bf16[16384,256]{1,0:T(8,128)(2,1)} async-done(((bf16[1024,256]{1,0:T(8,128)(2,1)}), bf16[16384,256]{1,0:T(8,128)(2,1)}) %all-gather.8.cloned.1.call-update) | async-done | bytes 8388624 | tf_op jit(solution)/shard_map/all_gather | solution.py:37
  330.7 1.8 fusion.9
  332.4 0.0 all-reduce.3.cloned.1.call-update
  332.5 0.2 reduce-scatter.2.cloned.1.call-start
  332.7 0.0 copy-start
  332.7 2.3 mul.21
  335.0 0.0 copy-done
  335.0 8.5 %fusion.4 = f32[1024,256]{1,0:T(8,128)} fusion(f32[128,8,16,128]{3,2,1,0:T(8,128)S(1)} %bitcast.13, s32[1024,2048]{1,0:T(8,128)} %param.7, bf16[1024,2048]{1,0:T(8,128)(2,1)S(1)} %copy-done, bf16[16384,256]{1,0:T(8,128)(2,1)} %all-gather.8.cloned.1.call-done, s32[]{:T(128)S(6)} %select_n.8), kind=kOutput, calls=%fused_computation.6 | convolution fusion | flops 1084227584 | bytes 23068676 | tf_op jit(solution)/shard_map/dot_general | solution.py:48
  343.5 0.0 reduce-scatter.2.cloned.1.call-update
  343.5 133.1 %all-reduce.3.cloned.1.call-done = f32[256,256]{1,0:T(8,128)} async-done(((f32[256,256]{1,0:T(8,128)}), f32[256,256]{1,0:T(8,128)}) %all-reduce.3.cloned.1.call-update) | async-done | bytes 262160 | tf_op jit(solution)/shard_map/psum | solution.py:46
  476.7 39.7 %reduce-scatter.2.cloned.1.call-done = f32[128,256]{1,0:T(8,128)} async-done(((f32[1024,256]{1,0:T(8,128)}), f32[128,256]{1,0:T(8,128)}) %reduce-scatter.2.cloned.1.call-update) | async-done | bytes 131088 | tf_op jit(solution)/shard_map/reduce_scatter | solution.py:47
  516.4 1.7 copy.19
Async XLA Ops:
  7.2 58.2 %all-gather.4.cloned.1.call-start = ((), (), s32[]{:S(2)}) async-start(), calls=%async_computation.2 | async-start | bytes 4718592 | tf_op jit(solution)/shard_map/all_gather | solution.py:16
  9.3 162.6 %all-gather.6.cloned.1.call-start = ((), (), s32[]{:S(2)}) async-start(), calls=%async_computation.3 | async-start | bytes 8912896 | tf_op jit(solution)/shard_map/all_gather | solution.py:20
  65.3 70.6 %all-to-all-start = ((bf16[128,16,1024]{0,2,1:T(8,128)(2,1)}), bf16[128,16,1024]{0,2,1:T(8,128)(2,1)}, u32[]{:S(2)}, u32[]{:S(2)}) async-start(bf16[128,16,1024]{0,2,1:T(8,128)(2,1)} %bitcast.14), calls=%async_computation | async-start | bytes 8388608 | tf_op jit(solution)/shard_map/all_to_all | solution.py:17
  72.0 258.6 %all-gather.8.cloned.1.call-start = ((), (), s32[]{:S(2)}) async-start(), calls=%async_computation.4 | async-start | bytes 8912896 | tf_op jit(solution)/shard_map/all_gather | solution.py:37
  186.2 72.5 %copy-start.1 = (f32[1024,16]{0,1:T(8,128)S(1)}, f32[1024,16]{0,1:T(8,128)}, u32[]{:S(2)}) copy-start(f32[1024,16]{0,1:T(8,128)} %param.8) | copy-start | bytes 196612
  258.6 218.1 %all-reduce.3.cloned.1.call-start = ((), (), s32[]{:S(2)}) async-start(), calls=%async_computation.6 | async-start | bytes 524288 | tf_op jit(solution)/shard_map/psum | solution.py:46
  332.5 183.9 %reduce-scatter.2.cloned.1.call-start = ((), (), s32[]{:S(2)}) async-start(), calls=%async_computation.5 | async-start | bytes 1179648 | tf_op jit(solution)/shard_map/reduce_scatter | solution.py:47
  332.7 2.3 copy-start
Sparse Core Ops, SparseCore 0:
  10.2 55.0 all-gather.3
  67.7 104.0 all-gather.5
  258.7 71.8 all-gather.7
  335.8 140.7 all-reduce.2
  479.5 36.8 reduce-scatter.1
where the time goes:
time: 525 us
  waiting for transfers between devices  394 us (75%)
  blocking collectives  67.2 us (13%)
  matrix products  29.9 us (6%)
  between operations  13.8 us (3%)
  local copies, waits for them, and re-layouts  12.6 us (2%)
  starting transfers between devices  7.09 us (1%)
    psum x1, waiting for transfers between devices, body(): gram = lax.psum(gram_part, ('wide', 'narrow'))  133 us
    all_gather x1, waiting for transfers between devices, body(): product_full = lax.all_gather(product_own, 'wide', axis=0, tiled=True)  71.8 us
    psum x1, blocking collectives, body(): product_own = lax.psum(partial_value, 'narrow').astype(jnp.bfloat16)  67.2 us
    all_to_all x1, waiting for transfers between devices, body(): lax.all_to_all(full_features, 'wide', split_axis=1, concat_axis=0, tiled=...  63.8 us
    all_gather x1, waiting for transfers between devices, body(): full_features = lax.all_gather(activations, 'narrow', axis=1, tiled=True)  55.3 us
    reduce_scatter x1, waiting for transfers between devices, body(): lax.psum_scatter(jnp.dot(residual, product_cols, preferred_element_type=j...  39.7 us
    all_gather x1, waiting for transfers between devices, body(): lax.all_gather(activations, 'wide', axis=0, tiled=True)  29.6 us
    dot_general x1, matrix products, body(): lax.dot_general(row_operand, lax.all_gather(activations, 'wide', axis=0,...  14.3 us
  transfers between devices with their start and end apart: 6, of which 6 were waited for; matrix products, arithmetic and copies ran while one was open for 3% of the time, Pallas kernels for 0%

commit v1 on v0

--- a/solution.py
+++ b/solution.py
@@ -33,7 +33,7 @@
     partial_value = jnp.dot(
         hessian, right_cols.astype(jnp.float32), precision=lax.Precision.HIGHEST
     )
-    product_own = lax.psum(partial_value, "narrow").astype(jnp.bfloat16)
+    product_own = jnp.sum(lax.all_gather(partial_value, "narrow"), axis=0).astype(jnp.bfloat16)
     product_full = lax.all_gather(product_own, "wide", axis=0, tiled=True)
     product_cols = lax.dynamic_slice_in_dim(product_full, narrow_index * cols_local, cols_local, 0)
     share = rows_local // narrow_count

time: 525 us -> 555 us (1.057)
  waiting for transfers between devices: 394 us -> 485 us
  blocking collectives: 67.2 us -> 0 us
    all_gather x0 -> x1, waiting for transfers between devices: none -> 91.6 us  [body(): lax.all_gather(partial_value, 'narrow')]
    psum x1 -> x0, blocking collectives: 67.2 us -> none  [body(): product_own = lax.psum(partial_value, 'narrow').astype(jnp.bfloat16)]
  transfers between devices with their start and end apart: 6 -> 7, of which waited for: 6 -> 7; matrix products, arithmetic and copies ran while one was open for 3% -> 3% of each run, Pallas kernels for 0% -> 0%
where the time goes in v1:
time: 555 us
  waiting for transfers between devices  485 us (87%)
  matrix products  30.9 us (6%)
  between operations  14.2 us (3%)
  local copies, waits for them, and re-layouts  12.5 us (2%)
  starting transfers between devices  7.13 us (1%)
    psum x1, waiting for transfers between devices, body(): gram = lax.psum(gram_part, ('wide', 'narrow'))  133 us
    all_gather x1, waiting for transfers between devices, body(): lax.all_gather(partial_value, 'narrow')  91.6 us
    all_gather x1, waiting for transfers between devices, body(): product_full = lax.all_gather(product_own, 'wide', axis=0, tiled=True)  71.4 us
    all_to_all x1, waiting for transfers between devices, body(): lax.all_to_all(full_features, 'wide', split_axis=1, concat_axis=0, tiled=...  63.8 us
    all_gather x1, waiting for transfers between devices, body(): full_features = lax.all_gather(activations, 'narrow', axis=1, tiled=True)  55.3 us
    reduce_scatter x1, waiting for transfers between devices, body(): lax.psum_scatter(jnp.dot(residual, product_cols, preferred_element_type=j...  39.7 us
    all_gather x1, waiting for transfers between devices, body(): lax.all_gather(activations, 'wide', axis=0, tiled=True)  29.6 us
    dot_general x1, matrix products, body(): lax.dot_general(row_operand, lax.all_gather(activations, 'wide', axis=0,...  14.3 us
  transfers between devices with their start and end apart: 7, of which 7 were waited for; matrix products, arithmetic and copies ran while one was open for 3% of the time, Pallas kernels for 0%

profile of v1, /device:TPU:0, one launch (start us, length us, event | category | flops | bytes accessed | tf_op | source)
XLA Modules:
  0.0 554.9 jit_solution(7533867203718450925)
XLA Ops:
  7.2 0.0 all-gather.6.cloned.1.call-start
  7.2 2.0 copy.11
  9.3 0.0 all-gather.6.cloned.1.call-update
  9.3 0.0 all-gather.8.cloned.1.call-start
  9.3 0.7 all-gather.8.cloned.1.call-update
  10.0 55.3 %all-gather.6.cloned.1.call-done = bf16[128,16384]{0,1:T(8,128)(2,1)} async-done(((bf16[128,2048]{0,1:T(8,128)(2,1)}), bf16[128,16384]{0,1:T(8,128)(2,1)}) %all-gather.6.cloned.1.call-update) | async-done | bytes 4194320 | tf_op jit(solution)/shard_map/all_gather | solution.py:16
  65.3 6.7 %all-to-all-start = ((bf16[128,16,1024]{0,2,1:T(8,128)(2,1)}), bf16[128,16,1024]{0,2,1:T(8,128)(2,1)}, u32[]{:S(2)}, u32[]{:S(2)}) async-start(bf16[128,16,1024]{0,2,1:T(8,128)(2,1)} %bitcast.16), calls=%async_computation | async-start | bytes 8388608 | tf_op jit(solution)/shard_map/all_to_all | solution.py:17
  72.0 0.0 all-gather.12.cloned.1.call-start
  72.1 63.8 %all-to-all-done = bf16[128,16,1024]{0,2,1:T(8,128)(2,1)} async-done(((bf16[128,16,1024]{0,2,1:T(8,128)(2,1)}), bf16[128,16,1024]{0,2,1:T(8,128)(2,1)}, u32[]{:S(2)}, u32[]{:S(2)}) %all-to-all-start) | async-done | bytes 4194336 | tf_op jit(solution)/shard_map/all_to_all | solution.py:17
  135.9 6.3 %copy.12 = bf16[16,128,1024]{2,1,0:T(8,128)(2,1)} copy(bf16[16,128,1024]{1,2,0:T(8,128)(2,1)} %bitcast.1) | data formatting | bytes 8388608 | tf_op jit(solution)/shard_map/all_to_all | solution.py:17
  142.2 29.6 %all-gather.8.cloned.1.call-done = bf16[2048,2048]{1,0:T(8,128)(2,1)} async-done(((bf16[128,2048]{1,0:T(8,128)(2,1)}), bf16[2048,2048]{1,0:T(8,128)(2,1)}) %all-gather.8.cloned.1.call-update) | async-done | bytes 8388624 | tf_op jit(solution)/shard_map/all_gather | solution.py:20
  171.8 14.3 %multiply_convert_fusion = (bf16[1024,2048]{1,0:T(8,128)(2,1)}, f32[1024,2048]{1,0:T(8,128)S(1)}) fusion(bf16[2048,1024]{1,0:T(8,128)(2,1)} %bitcast.17, bf16[2048,2048]{1,0:T(8,128)(2,1)} %all-gather.8.cloned.1.call-done), kind=kOutput, calls=%fused_computation.3 | convolution fusion | flops 8594128896 | bytes 25165824 | tf_op jit(solution)/shard_map/dot_general | solution.py:18
  186.2 6.3 %fusion.2 = f32[1024,256]{1,0:T(8,128)} fusion(f32[1024,2048]{1,0:T(8,128)S(1)} %get-tuple-element.4, bf16[16384,256]{1,0:T(8,128)(2,1)} %param.9, s32[]{:T(128)S(6)} %select_n.8), kind=kOutput, calls=%fused_computation.4 | convolution fusion | flops 6444548096 | bytes 10485764 | tf_op jit(solution)/shard_map/dot_general | solution.py:33
  192.4 0.0 copy-start.1
  192.4 0.0 all-gather.12.cloned.1.call-update
  192.5 0.0 all-gather.10.cloned.1.call-start
  192.5 91.6 %all-gather.12.cloned.1.call-done = f32[8192,256]{1,0:T(8,128)} async-done(((f32[1024,256]{1,0:T(8,128)}), f32[8192,256]{1,0:T(8,128)}) %all-gather.12.cloned.1.call-update) | async-done | bytes 8388624 | tf_op jit(solution)/shard_map/all_gather | solution.py:36
  284.1 4.9 reduce_sum.9
  289.0 0.0 all-gather.10.cloned.1.call-update
  289.0 0.0 all-reduce.2.cloned.1.call-start
  289.1 0.0 copy-done.1
  289.1 0.2 copy.10
  289.3 71.4 %all-gather.10.cloned.1.call-done = bf16[16384,256]{1,0:T(8,128)(2,1)} async-done(((bf16[1024,256]{1,0:T(8,128)(2,1)}), bf16[16384,256]{1,0:T(8,128)(2,1)}) %all-gather.10.cloned.1.call-update) | async-done | bytes 8388624 | tf_op jit(solution)/shard_map/all_gather | solution.py:37
  360.7 1.8 fusion.9
  362.4 0.0 all-reduce.2.cloned.1.call-update
  362.5 0.2 reduce-scatter.2.cloned.1.call-start
  362.7 0.0 copy-start
  362.7 2.3 mul.21
  365.0 0.0 copy-done
  365.0 8.5 %fusion.4 = f32[1024,256]{1,0:T(8,128)} fusion(f32[128,8,16,128]{3,2,1,0:T(8,128)S(1)} %bitcast.14, s32[1024,2048]{1,0:T(8,128)} %param.7, bf16[1024,2048]{1,0:T(8,128)(2,1)S(1)} %copy-done, bf16[16384,256]{1,0:T(8,128)(2,1)} %all-gather.10.cloned.1.call-done, s32[]{:T(128)S(6)} %select_n.8), kind=kOutput, calls=%fused_computation.6 | convolution fusion | flops 1084227584 | bytes 23068676 | tf_op jit(solution)/shard_map/dot_general | solution.py:48
  373.5 0.0 reduce-scatter.2.cloned.1.call-update
  373.5 133.1 %all-reduce.2.cloned.1.call-done = f32[256,256]{1,0:T(8,128)} async-done(((f32[256,256]{1,0:T(8,128)}), f32[256,256]{1,0:T(8,128)}) %all-reduce.2.cloned.1.call-update) | async-done | bytes 262160 | tf_op jit(solution)/shard_map/psum | solution.py:46
  506.7 39.7 %reduce-scatter.2.cloned.1.call-done = f32[128,256]{1,0:T(8,128)} async-done(((f32[1024,256]{1,0:T(8,128)}), f32[128,256]{1,0:T(8,128)}) %reduce-scatter.2.cloned.1.call-update) | async-done | bytes 131088 | tf_op jit(solution)/shard_map/reduce_scatter | solution.py:47
  546.4 1.7 copy.17
Async XLA Ops:
  7.2 58.2 %all-gather.6.cloned.1.call-start = ((), (), s32[]{:S(2)}) async-start(), calls=%async_computation.2 | async-start | bytes 4718592 | tf_op jit(solution)/shard_map/all_gather | solution.py:16
  9.3 162.6 %all-gather.8.cloned.1.call-start = ((), (), s32[]{:S(2)}) async-start(), calls=%async_computation.3 | async-start | bytes 8912896 | tf_op jit(solution)/shard_map/all_gather | solution.py:20
  65.3 70.6 %all-to-all-start = ((bf16[128,16,1024]{0,2,1:T(8,128)(2,1)}), bf16[128,16,1024]{0,2,1:T(8,128)(2,1)}, u32[]{:S(2)}, u32[]{:S(2)}) async-start(bf16[128,16,1024]{0,2,1:T(8,128)(2,1)} %bitcast.16), calls=%async_computation | async-start | bytes 8388608 | tf_op jit(solution)/shard_map/all_to_all | solution.py:17
  72.0 212.0 %all-gather.12.cloned.1.call-start = ((), (), s32[]{:S(2)}) async-start(), calls=%async_computation.7 | async-start | bytes 9437184 | tf_op jit(solution)/shard_map/all_gather | solution.py:36
  192.4 96.6 %copy-start.1 = (f32[1024,16]{0,1:T(8,128)S(1)}, f32[1024,16]{0,1:T(8,128)}, u32[]{:S(2)}) copy-start(f32[1024,16]{0,1:T(8,128)} %param.8) | copy-start | bytes 196612
  192.5 168.2 %all-gather.10.cloned.1.call-start = ((), (), s32[]{:S(2)}) async-start(), calls=%async_computation.4 | async-start | bytes 8912896 | tf_op jit(solution)/shard_map/all_gather | solution.py:37
  289.0 217.6 %all-reduce.2.cloned.1.call-start = ((), (), s32[]{:S(2)}) async-start(), calls=%async_computation.6 | async-start | bytes 524288 | tf_op jit(solution)/shard_map/psum | solution.py:46
  362.5 183.9 %reduce-scatter.2.cloned.1.call-start = ((), (), s32[]{:S(2)}) async-start(), calls=%async_computation.5 | async-start | bytes 1179648 | tf_op jit(solution)/shard_map/reduce_scatter | solution.py:47
  362.7 2.3 copy-start
Sparse Core Ops, SparseCore 0:
  10.2 55.0 all-gather.5
  67.7 104.0 all-gather.7
  192.6 91.4 all-gather.11
  289.2 71.4 all-gather.9
  365.8 140.7 all-reduce.1
  509.5 36.8 reduce-scatter.1
